TPU v7x, 256 devices: a whole 4x4x8 slice. The times are simulated.
256 devices in a mesh: row: 16 (over y_lo, x, core), col: 16 (over y_hi, z).
Axes of the slice: x: 4, y: 4 (y_hi: 2, y_lo: 2; y = y_hi * 2 + y_lo), z: 8, core: 2. Of those that a mesh axis runs over, the one named last changes fastest.
Arguments:
- val_orb: bfloat16 [64, 2048], replicated, may hold values from -6 to 6
- con_orb: bfloat16 [512, 2048], replicated, may hold values from -6 to 6
- val_energy: float32 [64], replicated, may hold values from -1.5 to -0.5
- con_energy: float32 [512], replicated, may hold values from 0.5 to 2
- points: int32 [1024], replicated, may hold values from 0 to 2047, as said below
- val_band: int32 [1048576], P(('row', 'col')), may hold values from 0 to 63
- con_band: int32 [1048576], P(('row', 'col')), may hold values from 0 to 511
- kernel: bfloat16 [1024, 1024], replicated
- trial_vecs: bfloat16 [1048576, 128], P(('row', 'col')), may hold values from -6 to 6
Outputs:
- first_degree: bfloat16 [1048576, 128], P(('row', 'col'))
- filtered: float32 [1048576, 128], P(('row', 'col'))
Inputs may be any that keep to these rules, and one draw needn't show every extreme that they name: Distinct grid points.
All inputs are finite; a program needn't handle non-finite values.
Results may differ from a plain program's by a relative error of at most 0.0042.
Values sent between devices are 32-bit elements; how exact they have to be, the bound alone decides.
A program may use at most 128 MiB of HBM per device.

v0:
```python
import jax
import jax.numpy as jnp
from jax import lax
from jax.sharding import PartitionSpec as P

filter_center = 2.25
filter_half = 1.25


def factor_rows(val_points, con_points, val_band, con_band):
    product = jnp.take(val_points, val_band, axis=0).astype(jnp.float32) * jnp.take(
        con_points, con_band, axis=0
    ).astype(jnp.float32)
    return product.astype(jnp.bfloat16)


def shards(
    val_orb, con_orb, val_energy, con_energy, points, val_band, con_band, kernel, trial_vecs
):
    val_points = jnp.take(val_orb, points, axis=1)
    con_points = jnp.take(con_orb, points, axis=1)
    energy = (jnp.take(con_energy, con_band) - jnp.take(val_energy, val_band))[:, None]
    own_rows = factor_rows(val_points, con_points, val_band, con_band)
    kernel_wide = kernel.astype(jnp.float32)
    rows_wide = own_rows.astype(jnp.float32)

    def apply_kernel(vectors):
        partial_proj = lax.dot_general(
            own_rows, vectors, (((0,), (0,)), ((), ())), preferred_element_type=jnp.float32
        )
        projected = lax.psum(partial_proj, ("row", "col"))
        mixed = jnp.dot(kernel_wide, projected, precision=lax.Precision.HIGHEST)
        return jnp.dot(rows_wide, mixed, precision=lax.Precision.HIGHEST)

    start_vecs = trial_vecs.astype(jnp.float32)
    first = ((energy - filter_center) * start_vecs + apply_kernel(trial_vecs)) / filter_half
    first_degree = first.astype(jnp.bfloat16)
    first_wide = first_degree.astype(jnp.float32)
    filtered = (
        2.0 * ((energy - filter_center) * first_wide + apply_kernel(first_degree)) / filter_half
        - start_vecs
    )
    return (first_degree, filtered)


def solution(mesh):
    placed = (
        P(),
        P(),
        P(),
        P(),
        P(),
        P(("row", "col")),
        P(("row", "col")),
        P(),
        P(("row", "col"), None),
    )
    return jax.shard_map(
        shards,
        mesh=mesh,
        in_specs=placed,
        out_specs=(P(("row", "col"), None), P(("row", "col"), None)),
        check_vma=False,
    )
```

profile of v0, /device:TPU:2, one launch (start us, length us, event | category | flops | bytes accessed | tf_op | source)
XLA Modules:
  0.0 709.2 jit_solution(5484198504451303308)
XLA Ops:
  7.2 0.0 copy-start
  7.2 0.0 all-reduce.3.cloned.1.call-start
  7.2 0.8 fusion.8
  8.1 0.7 compare_and_fusion.2
  8.8 1.6 fusion.12
  10.3 2.1 fusion.9
  12.4 2.1 fusion.10
  14.5 2.1 fusion.11
  16.6 1.3 fusion.7
  17.9 1.3 compare_and_fusion
  19.2 4.0 copy.17
  23.2 5.8 gather_fusion.3
  29.0 1.2 select_bitcast_fusion
  30.2 1.5 copy.18
  31.7 0.0 copy-done.11
  31.7 0.0 copy-done.5
  31.8 1.0 copy.15
  32.8 5.2 gather_fusion.1
  38.0 1.2 select_bitcast_fusion.1
  39.1 0.1 copy.16
  39.2 0.0 copy-start.1
  39.3 18.3 %gather_fusion.4 = bf16[4096,1024]{1,0:T(8,128)(2,1)} fusion(bf16[512,1024]{1,0:T(8,128)(2,1)S(1)} %copy.18, s32[4096]{0:T(1024)S(1)} %fusion.6), kind=kCustom, calls=%fused_computation.4 | custom fusion | bytes 16793600 | tf_op jit(solution)/shard_map/jit(_take)/gather | solution.py:11
  57.5 0.0 copy-done.1
  57.5 25.9 %gather_fusion = f32[4096]{0:T(1024)S(1)} fusion(f32[512]{0:T(512)S(1)} %copy-done.1, s32[4096]{0:T(1024)S(1)} %fusion.6), kind=kCustom, calls=%fused_computation | custom fusion | bytes 49152 | tf_op jit(solution)/shard_map/jit(_take)/gather | solution.py:22
  83.4 0.0 copy-start.6
  83.4 0.0 copy-start.9
  83.4 0.0 copy-start.10
  83.5 18.3 %gather_fusion.2 = bf16[4096,1024]{1,0:T(8,128)(2,1)} fusion(bf16[64,1024]{1,0:T(8,128)(2,1)S(1)} %copy.16, s32[4096]{0:T(1024)S(1)} %copy-done.7), kind=kCustom, calls=%fused_computation.2 | custom fusion | bytes 16793600 | tf_op jit(solution)/shard_map/jit(_take)/gather | solution.py:11
  101.7 0.0 copy-done.6
  101.7 40.1 %fusion.5 = (f32[4096]{0:T(1024)S(1)}, pred[4096]{0:T(1024)(128)(4,1)S(1)}) fusion(f32[4096]{0:T(1024)S(1)} %gather_fusion, s32[4096]{0:T(1024)S(1)} %copy-done.6, f32[]{:T(128)} %bitcast, f32[]{:T(128)} %bitcast.1, f32[]{:T(128)} %bitcast.2, f32[]{:T(128)} %bitcast.3, f32[]{:T(128)} %bitcast.4, f32[]{:T(128)} %bitcast.5, f32[]{:T(128)} %bitcast.6, ...), kind=kLoop, calls=%fused_computation.19 | loop fusion | flops 581632 | bytes 69888 | tf_op jit(solution)/shard_map/sub | solution.py:36
  141.8 0.0 copy-start.3
  141.8 7.7 %multiply_convert_fusion = bf16[4096,1024]{1,0:T(8,128)(2,1)S(1)} fusion(bf16[4096,1024]{1,0:T(8,128)(2,1)} %gather_fusion.4, bf16[4096,1024]{1,0:T(8,128)(2,1)} %gather_fusion.2, pred[4096]{0:T(1024)(128)(4,1)S(1)} %get-tuple-element.3, pred[4096]{0:T(1024)(128)(4,1)S(1)} %copy-done.10), kind=kLoop, calls=%fused_computation.5 | loop fusion | flops 25165824 | bytes 25174016 | tf_op jit(solution)/shard_map/convert_element_type | solution.py:14
  149.5 0.0 copy-start.2
  149.5 3.2 copy-done.2
  152.8 3.1 fusion.13
  155.9 0.0 all-reduce.3.cloned.1.call-update
  155.9 0.0 all-reduce.5.cloned.1.call-start
  156.0 258.4 %all-reduce.3.cloned.1.call-done = f32[1024,128]{1,0:T(8,128)} async-done(((f32[1024,128]{1,0:T(8,128)}), f32[1024,128]{1,0:T(8,128)}) %all-reduce.3.cloned.1.call-update) | async-done | bytes 524304 | tf_op jit(solution)/shard_map/psum | solution.py:31
  414.4 0.0 copy-done
  414.4 3.3 fusion.14
  417.8 9.3 %fusion.3 = bf16[4096,128]{1,0:T(8,128)(2,1)S(1)} fusion(bf16[4096,1024]{1,0:T(8,128)(2,1)} %copy-done.2, f32[128,1024]{1,0:T(8,128)S(1)} %fusion.14, bf16[4096,128]{1,0:T(8,128)(2,1)S(1)} %copy-done.3, f32[4096]{0:T(1024)S(1)} %get-tuple-element.2), kind=kOutput, calls=%fused_computation.11 | convolution fusion | flops 6445072384 | bytes 11026432 | tf_op jit(solution)/shard_map/dot_general | solution.py:33
  427.1 0.0 copy-start.4
  427.1 1.0 copy-done.4
  428.0 6.6 fusion.15
  434.6 0.0 all-reduce.5.cloned.1.call-update
  434.6 254.2 %all-reduce.5.cloned.1.call-done = f32[1024,128]{1,0:T(8,128)} async-done(((f32[1024,128]{1,0:T(8,128)}), f32[1024,128]{1,0:T(8,128)}) %all-reduce.5.cloned.1.call-update) | async-done | bytes 524304 | tf_op jit(solution)/shard_map/psum | solution.py:31
  688.8 3.3 fusion.16
  692.2 10.2 %fusion.1 = f32[4096,128]{1,0:T(8,128)} fusion(bf16[4096,1024]{1,0:T(8,128)(2,1)} %copy-done.2, f32[128,1024]{1,0:T(8,128)S(1)} %fusion.16, bf16[4096,128]{1,0:T(8,128)(2,1)S(1)} %copy-done.3, bf16[4096,128]{1,0:T(8,128)(2,1)} %copy-done.4, f32[4096]{0:T(1024)S(1)} %get-tuple-element.2), kind=kOutput, calls=%fused_computation.8 | convolution fusion | flops 6445596672 | bytes 13123584 | tf_op jit(solution)/shard_map/dot_general | solution.py:33
  (10 shorter events, 0.0 us)
Async XLA Ops:
  7.2 407.3 %copy-start = (bf16[1024,1024]{1,0:T(8,128)(2,1)S(1)}, bf16[1024,1024]{1,0:T(8,128)(2,1)}, u32[]{:S(2)}) copy-start(bf16[1024,1024]{1,0:T(8,128)(2,1)} %param.16) | copy-start | bytes 6291460
  7.2 407.3 %all-reduce.3.cloned.1.call-start = ((), (), s32[]{:S(2)}) async-start(), calls=%async_computation | async-start | bytes 1048576 | tf_op jit(solution)/shard_map/psum | solution.py:31
  8.8 23.0 %copy-start.11 = (pred[1024]{0:T(1024)(128)(4,1)}, pred[1024]{0:T(1024)(128)(4,1)S(1)}, u32[]{:S(2)}) copy-start(pred[1024]{0:T(1024)(128)(4,1)S(1)} %compare_and_fusion.2) | copy-start | bytes 3076
  19.2 12.5 %copy-start.8 = (s32[4096]{0:T(1024)S(1)}, s32[4096]{0:T(1024)}, u32[]{:S(2)}) copy-start(s32[4096]{0:T(1024)} %param.15) | copy-start | bytes 49156
  19.2 12.5 %copy-start.5 = (bf16[64,2048]{1,0:T(8,128)(2,1)S(1)}, bf16[64,2048]{1,0:T(8,128)(2,1)}, u32[]{:S(2)}) copy-start(bf16[64,2048]{1,0:T(8,128)(2,1)} %param.9) | copy-start | bytes 786436
  39.2 18.3 %copy-start.1 = (f32[512]{0:T(512)S(1)}, f32[512]{0:T(512)}, u32[]{:S(2)}) copy-start(f32[512]{0:T(512)} %param.12) | copy-start | bytes 6148
  57.5 25.9 %copy-start.7 = (s32[4096]{0:T(1024)S(1)}, s32[4096]{0:T(1024)}, u32[]{:S(2)}) copy-start(s32[4096]{0:T(1024)} %fusion.7) | copy-start | bytes 49156
  83.4 18.3 %copy-start.6 = (s32[4096]{0:T(1024)S(1)}, s32[4096]{0:T(1024)}, u32[]{:S(2)}) copy-start(s32[4096]{0:T(1024)} %param.14) | copy-start | bytes 49156
  83.4 18.3 %copy-start.9 = (s32[4096]{0:T(1024)S(1)}, s32[4096]{0:T(1024)}, u32[]{:S(2)}) copy-start(s32[4096]{0:T(1024)} %param.15) | copy-start | bytes 49156
  83.4 58.3 %copy-start.10 = (pred[4096]{0:T(1024)(128)(4,1)S(1)}, pred[4096]{0:T(1024)(128)(4,1)}, u32[]{:S(2)}) copy-start(pred[4096]{0:T(1024)(128)(4,1)} %compare_and_fusion) | copy-start | bytes 12292
  141.8 11.0 %copy-start.3 = (bf16[4096,128]{1,0:T(8,128)(2,1)S(1)}, bf16[4096,128]{1,0:T(8,128)(2,1)}, u32[]{:S(2)}) copy-start(bf16[4096,128]{1,0:T(8,128)(2,1)} %param.17) | copy-start | bytes 3145732
  149.5 3.2 copy-start.2
  155.9 532.9 %all-reduce.5.cloned.1.call-start = ((), (), s32[]{:S(2)}) async-start(), calls=%async_computation.1 | async-start | bytes 1048576 | tf_op jit(solution)/shard_map/psum | solution.py:31
  427.1 1.0 copy-start.4
Sparse Core Ops, SparseCore 0:
  156.1 258.3 all-reduce.2
  434.7 254.0 all-reduce.4
where the time goes:
time: 710 us; the launch traced here: 709 us
  waiting for transfers between devices  513 us (72%)
  local copies, waits for them, and re-layouts  92.1 us (13%)
  other arithmetic  54.3 us (8%)
  matrix products  35.8 us (5%)
  between operations  14.2 us (2%)
    psum x2, waiting for transfers between devices, apply_kernel(): projected = lax.psum(partial_proj, ('row', 'col'))  513 us
    sub x1, other arithmetic, shards(): energy - filter_center  40.1 us
    gather x1, local copies, waits for them, and re-layouts, shards(): jnp.take(con_energy, con_band) - jnp.take(val_energy, val_band)  25.9 us
    dot_general x2, matrix products, apply_kernel(): return jnp.dot(rows_wide, mixed, precision=lax.Precision.HIGHEST)  19.5 us
    gather x1, local copies, waits for them, and re-layouts, factor_rows(): jnp.take(con_points, con_band, axis=0).astype(jnp.float32)  18.3 us
    gather x1, local copies, waits for them, and re-layouts, factor_rows(): jnp.take(val_points, val_band, axis=0).astype(jnp.float32)  18.3 us
  transfers between devices with their start and end apart: 2, of which 2 were waited for; matrix products, arithmetic and copies ran while one was open for 0% of the time, Pallas kernels for 0%

commit v1 on v0

--- a/solution.py
+++ b/solution.py
@@ -28,7 +28,7 @@
         partial_proj = lax.dot_general(
             own_rows, vectors, (((0,), (0,)), ((), ())), preferred_element_type=jnp.float32
         )
-        projected = lax.psum(partial_proj, ("row", "col"))
+        projected = lax.psum(lax.psum(partial_proj, "row"), "col")
         mixed = jnp.dot(kernel_wide, projected, precision=lax.Precision.HIGHEST)
         return jnp.dot(rows_wide, mixed, precision=lax.Precision.HIGHEST)
 

time: 710 us -> 768 us (1.082)
  waiting for transfers between devices: 513 us -> 570 us
    psum x2 -> x4, waiting for transfers between devices: 513 us -> 570 us  [apply_kernel(): projected = lax.psum(lax.psum(partial_proj, 'row'), 'col')]
  transfers between devices with their start and end apart: 2 -> 4, of which waited for: 2 -> 4; matrix products, arithmetic and copies ran while one was open for 0% -> 0% of each run, Pallas kernels for 0% -> 0%
where the time goes in v1:
time: 768 us; the launch traced here: 767 us
  waiting for transfers between devices  570 us (74%)
  local copies, waits for them, and re-layouts  92.1 us (12%)
  other arithmetic  54.3 us (7%)
  matrix products  35.6 us (5%)
  between operations  14 us (2%)
    psum x4, waiting for transfers between devices, apply_kernel(): projected = lax.psum(lax.psum(partial_proj, 'row'), 'col')  570 us
    sub x1, other arithmetic, shards(): energy - filter_center  40.1 us
    gather x1, local copies, waits for them, and re-layouts, shards(): jnp.take(con_energy, con_band) - jnp.take(val_energy, val_band)  25.9 us
    dot_general x2, matrix products, apply_kernel(): return jnp.dot(rows_wide, mixed, precision=lax.Precision.HIGHEST)  19.3 us
    gather x1, local copies, waits for them, and re-layouts, factor_rows(): jnp.take(con_points, con_band, axis=0).astype(jnp.float32)  18.3 us
    gather x1, local copies, waits for them, and re-layouts, factor_rows(): jnp.take(val_points, val_band, axis=0).astype(jnp.float32)  18.3 us
  transfers between devices with their start and end apart: 4, of which 4 were waited for; matrix products, arithmetic and copies ran while one was open for 0% of the time, Pallas kernels for 0%

profile of v1, /device:TPU:2, one launch (start us, length us, event | category | flops | bytes accessed | tf_op | source)
XLA Modules:
  0.0 766.7 jit_solution(5335626166822628948)
XLA Ops:
  7.2 0.0 copy-start
  7.2 0.0 all-reduce.5.cloned.1.call-start
  7.2 0.8 fusion.8
  8.1 0.7 compare_and_fusion.2
  8.8 1.6 fusion.12
  10.3 2.1 fusion.9
  12.4 2.1 fusion.10
  14.5 2.1 fusion.11
  16.6 1.3 fusion.7
  17.9 1.3 compare_and_fusion
  19.2 4.0 copy.17
  23.2 5.8 gather_fusion.3
  29.0 1.2 select_bitcast_fusion
  30.2 1.5 copy.18
  31.7 0.0 copy-done.5
  31.8 1.0 copy.15
  32.8 5.2 gather_fusion.1
  38.0 1.2 select_bitcast_fusion.1
  39.1 0.1 copy.16
  39.2 0.0 copy-start.1
  39.3 18.3 %gather_fusion.4 = bf16[4096,1024]{1,0:T(8,128)(2,1)} fusion(bf16[512,1024]{1,0:T(8,128)(2,1)S(1)} %copy.18, s32[4096]{0:T(1024)S(1)} %fusion.6), kind=kCustom, calls=%fused_computation.4 | custom fusion | bytes 16793600 | tf_op jit(solution)/shard_map/jit(_take)/gather | solution.py:11
  57.5 25.9 %gather_fusion = f32[4096]{0:T(1024)S(1)} fusion(f32[512]{0:T(512)S(1)} %copy-done.1, s32[4096]{0:T(1024)S(1)} %fusion.6), kind=kCustom, calls=%fused_computation | custom fusion | bytes 49152 | tf_op jit(solution)/shard_map/jit(_take)/gather | solution.py:22
  83.4 0.0 copy-start.6
  83.4 0.0 copy-start.9
  83.5 18.3 %gather_fusion.2 = bf16[4096,1024]{1,0:T(8,128)(2,1)} fusion(bf16[64,1024]{1,0:T(8,128)(2,1)S(1)} %copy.16, s32[4096]{0:T(1024)S(1)} %copy-done.7), kind=kCustom, calls=%fused_computation.2 | custom fusion | bytes 16793600 | tf_op jit(solution)/shard_map/jit(_take)/gather | solution.py:11
  101.7 40.1 %fusion.5 = (f32[4096]{0:T(1024)S(1)}, pred[4096]{0:T(1024)(128)(4,1)S(1)}) fusion(f32[4096]{0:T(1024)S(1)} %gather_fusion, s32[4096]{0:T(1024)S(1)} %copy-done.6, f32[]{:T(128)} %bitcast, f32[]{:T(128)} %bitcast.1, f32[]{:T(128)} %bitcast.2, f32[]{:T(128)} %bitcast.3, f32[]{:T(128)} %bitcast.4, f32[]{:T(128)} %bitcast.5, f32[]{:T(128)} %bitcast.6, ...), kind=kLoop, calls=%fused_computation.19 | loop fusion | flops 581632 | bytes 69888 | tf_op jit(solution)/shard_map/sub | solution.py:36
  141.8 0.0 copy-start.3
  141.8 7.7 %multiply_convert_fusion = bf16[4096,1024]{1,0:T(8,128)(2,1)S(1)} fusion(bf16[4096,1024]{1,0:T(8,128)(2,1)} %gather_fusion.4, bf16[4096,1024]{1,0:T(8,128)(2,1)} %gather_fusion.2, pred[4096]{0:T(1024)(128)(4,1)S(1)} %get-tuple-element.3, pred[4096]{0:T(1024)(128)(4,1)S(1)} %copy-done.10), kind=kLoop, calls=%fused_computation.5 | loop fusion | flops 25165824 | bytes 25174016 | tf_op jit(solution)/shard_map/convert_element_type | solution.py:14
  149.5 3.2 copy-done.2
  152.8 3.1 fusion.13
  155.9 0.0 all-reduce.5.cloned.1.call-update
  155.9 0.0 all-reduce.7.cloned.1.call-start
  156.0 123.6 %all-reduce.5.cloned.1.call-done = f32[1024,128]{1,0:T(8,128)} async-done(((f32[1024,128]{1,0:T(8,128)}), f32[1024,128]{1,0:T(8,128)}) %all-reduce.5.cloned.1.call-update) | async-done | bytes 524304 | tf_op jit(solution)/shard_map/psum | solution.py:31
  279.6 0.0 all-reduce.7.cloned.1.call-update
  279.6 0.2 all-reduce.9.cloned.1.call-start
  279.9 164.3 %all-reduce.7.cloned.1.call-done = f32[1024,128]{1,0:T(8,128)} async-done(((f32[1024,128]{1,0:T(8,128)}), f32[1024,128]{1,0:T(8,128)}) %all-reduce.7.cloned.1.call-update) | async-done | bytes 524304 | tf_op jit(solution)/shard_map/psum | solution.py:31
  444.1 3.3 fusion.14
  447.5 9.1 %fusion.3 = bf16[4096,128]{1,0:T(8,128)(2,1)S(1)} fusion(bf16[4096,1024]{1,0:T(8,128)(2,1)} %copy-done.2, f32[128,1024]{1,0:T(8,128)S(1)} %fusion.14, bf16[4096,128]{1,0:T(8,128)(2,1)S(1)} %copy-done.3, f32[4096]{0:T(1024)S(1)} %get-tuple-element.2), kind=kOutput, calls=%fused_computation.11 | convolution fusion | flops 6445072384 | bytes 11026432 | tf_op jit(solution)/shard_map/dot_general | solution.py:33
  456.6 0.0 copy-start.4
  456.6 1.0 copy-done.4
  457.6 6.6 fusion.15
  464.1 0.0 all-reduce.9.cloned.1.call-update
  464.1 0.3 all-reduce.11.cloned.1.call-start
  464.4 117.9 %all-reduce.9.cloned.1.call-done = f32[1024,128]{1,0:T(8,128)} async-done(((f32[1024,128]{1,0:T(8,128)}), f32[1024,128]{1,0:T(8,128)}) %all-reduce.9.cloned.1.call-update) | async-done | bytes 524304 | tf_op jit(solution)/shard_map/psum | solution.py:31
  582.3 0.0 all-reduce.11.cloned.1.call-update
  582.3 164.4 %all-reduce.11.cloned.1.call-done = f32[1024,128]{1,0:T(8,128)} async-done(((f32[1024,128]{1,0:T(8,128)}), f32[1024,128]{1,0:T(8,128)}) %all-reduce.11.cloned.1.call-update) | async-done | bytes 524304 | tf_op jit(solution)/shard_map/psum | solution.py:31
  746.7 3.3 fusion.16
  750.0 10.2 %fusion.1 = f32[4096,128]{1,0:T(8,128)} fusion(bf16[4096,1024]{1,0:T(8,128)(2,1)} %copy-done.2, f32[128,1024]{1,0:T(8,128)S(1)} %fusion.16, bf16[4096,128]{1,0:T(8,128)(2,1)S(1)} %copy-done.3, bf16[4096,128]{1,0:T(8,128)(2,1)} %copy-done.4, f32[4096]{0:T(1024)S(1)} %get-tuple-element.2), kind=kOutput, calls=%fused_computation.8 | convolution fusion | flops 6445596672 | bytes 13123584 | tf_op jit(solution)/shard_map/dot_general | solution.py:33
  (16 shorter events, 0.0 us)
Async XLA Ops:
  7.2 437.0 %copy-start = (bf16[1024,1024]{1,0:T(8,128)(2,1)S(1)}, bf16[1024,1024]{1,0:T(8,128)(2,1)}, u32[]{:S(2)}) copy-start(bf16[1024,1024]{1,0:T(8,128)(2,1)} %param.16) | copy-start | bytes 6291460
  7.2 272.4 %all-reduce.5.cloned.1.call-start = ((), (), s32[]{:S(2)}) async-start(), calls=%async_computation | async-start | bytes 1048576 | tf_op jit(solution)/shard_map/psum | solution.py:31
  8.8 23.0 %copy-start.11 = (pred[1024]{0:T(1024)(128)(4,1)}, pred[1024]{0:T(1024)(128)(4,1)S(1)}, u32[]{:S(2)}) copy-start(pred[1024]{0:T(1024)(128)(4,1)S(1)} %compare_and_fusion.2) | copy-start | bytes 3076
  19.2 12.5 %copy-start.8 = (s32[4096]{0:T(1024)S(1)}, s32[4096]{0:T(1024)}, u32[]{:S(2)}) copy-start(s32[4096]{0:T(1024)} %param.15) | copy-start | bytes 49156
  19.2 12.5 %copy-start.5 = (bf16[64,2048]{1,0:T(8,128)(2,1)S(1)}, bf16[64,2048]{1,0:T(8,128)(2,1)}, u32[]{:S(2)}) copy-start(bf16[64,2048]{1,0:T(8,128)(2,1)} %param.9) | copy-start | bytes 786436
  39.2 18.3 %copy-start.1 = (f32[512]{0:T(512)S(1)}, f32[512]{0:T(512)}, u32[]{:S(2)}) copy-start(f32[512]{0:T(512)} %param.12) | copy-start | bytes 6148
  57.5 25.9 %copy-start.7 = (s32[4096]{0:T(1024)S(1)}, s32[4096]{0:T(1024)}, u32[]{:S(2)}) copy-start(s32[4096]{0:T(1024)} %fusion.7) | copy-start | bytes 49156
  83.4 18.3 %copy-start.6 = (s32[4096]{0:T(1024)S(1)}, s32[4096]{0:T(1024)}, u32[]{:S(2)}) copy-start(s32[4096]{0:T(1024)} %param.14) | copy-start | bytes 49156
  83.4 18.3 %copy-start.9 = (s32[4096]{0:T(1024)S(1)}, s32[4096]{0:T(1024)}, u32[]{:S(2)}) copy-start(s32[4096]{0:T(1024)} %param.15) | copy-start | bytes 49156
  83.4 58.3 %copy-start.10 = (pred[4096]{0:T(1024)(128)(4,1)S(1)}, pred[4096]{0:T(1024)(128)(4,1)}, u32[]{:S(2)}) copy-start(pred[4096]{0:T(1024)(128)(4,1)} %compare_and_fusion) | copy-start | bytes 12292
  141.8 11.0 %copy-start.3 = (bf16[4096,128]{1,0:T(8,128)(2,1)S(1)}, bf16[4096,128]{1,0:T(8,128)(2,1)}, u32[]{:S(2)}) copy-start(bf16[4096,128]{1,0:T(8,128)(2,1)} %param.17) | copy-start | bytes 3145732
  149.5 3.2 copy-start.2
  155.9 288.2 %all-reduce.7.cloned.1.call-start = ((), (), s32[]{:S(2)}) async-start(), calls=%async_computation.1 | async-start | bytes 1048576 | tf_op jit(solution)/shard_map/psum | solution.py:31
  279.6 302.7 %all-reduce.9.cloned.1.call-start = ((), (), s32[]{:S(2)}) async-start(), calls=%async_computation.2 | async-start | bytes 1048576 | tf_op jit(solution)/shard_map/psum | solution.py:31
  456.6 1.0 copy-start.4
  464.1 282.5 %all-reduce.11.cloned.1.call-start = ((), (), s32[]{:S(2)}) async-start(), calls=%async_computation.3 | async-start | bytes 1048576 | tf_op jit(solution)/shard_map/psum | solution.py:31
Sparse Core Ops, SparseCore 0:
  156.1 123.5 all-reduce.4
  282.2 161.8 all-reduce.6
  464.3 117.9 all-reduce.8
  584.8 161.8 all-reduce.10
